TPU v7x, 256 devices: a whole 4x4x8 slice. The times are simulated.
256 devices in a mesh: bubble: 16 (over y_hi, z), panel: 16 (over y_lo, x, core).
Axes of the slice: x: 4, y: 4 (y_hi: 2, y_lo: 2; y = y_hi * 2 + y_lo), z: 8, core: 2. Of those that a mesh axis runs over, the one named last changes fastest.
Arguments:
- density: float32 [128, 12288], P('bubble', 'panel'), may hold values from -6 to 6
- right_side: float32 [128, 12288], P('bubble', 'panel'), may hold values from -6 to 6
- inv_diag: bfloat16 [128, 96, 128, 128], P('bubble', 'panel')
- near_vals: bfloat16 [128, 96, 4, 128, 128], P('bubble', 'panel'), may hold values from -0.25 to 0.25
- near_bubble: int32 [128, 96, 4], P('bubble', 'panel'), may hold values from 0 to 127, as said below
- near_block: int32 [128, 96, 4], P('bubble', 'panel'), may hold values from 0 to 95
- near_count: int32 [128, 96], P('bubble', 'panel'), may hold values from 1 to 4, as said below
- colour: int32 [128], P('bubble'), may hold values from 0 to 1
- moment_map: bfloat16 [128, 16, 12288], P('bubble', None, 'panel'), may hold values from -0.0546875 to 0.0546875
- spread_map: bfloat16 [128, 16, 12288], P('bubble', None, 'panel'), may hold values from -0.125 to 0.125
- centres: float32 [3, 128], replicated, may hold values from 0.2 to 6
Outputs:
- relaxed: float32 [128, 12288], P('bubble', 'panel')
Inputs may be any that keep to these rules, and one draw needn't show every extreme that they name: `near_bubble`: every slot of bubble b names a bubble within 8 of b. `near_count`: the first row block of every bubble uses all 4 slots.
All inputs are finite; a program needn't handle non-finite values.
Results may differ from a plain program's by a relative error of at most 0.0041.
Values may be sent and summed in bfloat16 or wider, within the bound.
No kernel may reach another device: no remote copies, remote signals or barrier semaphores. Data moves between devices by JAX's collectives and lax.ppermute only.
A program may use at most 64 MiB of HBM per device.

v0:
```python
import jax
import jax.numpy as jnp
from jax import lax
from jax.sharding import PartitionSpec as P


def with_halo(shard, sides, width):
    for axis, dim in sides:
        peers, length = (lax.axis_size(axis), shard.shape[dim])
        up = [(i, (i + 1) % peers) for i in range(peers - 1)]
        down = [(j, i) for i, j in up]
        last = lax.slice_in_dim(shard, length - width, length, axis=dim)
        first = lax.slice_in_dim(shard, 0, width, axis=dim)
        before = lax.ppermute(last, axis, up)
        after = lax.ppermute(first, axis, down)
        shard = jnp.concatenate([before, shard, after], axis=dim)
    return shard


def near_field(
    neighbourhood, near_vals, near_bubble, near_block, near_count, first_bubble, block_size
):
    rim_count = neighbourhood.shape[0]
    blocks = neighbourhood.reshape(rim_count, neighbourhood.shape[1] // block_size, block_size)
    local_bubble = near_bubble - first_bubble
    sources = blocks[local_bubble, near_block]
    live_slot = jnp.arange(near_vals.shape[2])[None, None, :] < near_count[:, :, None]
    sources = jnp.where(live_slot[:, :, :, None], sources, jnp.zeros_like(sources))
    return jnp.einsum("brsij,brsj->bri", near_vals, sources, preferred_element_type=jnp.float32)


def far_kernel(centres, my_bubbles, reach):
    centre_mine = centres[:, my_bubbles]
    diff = centre_mine[:, :, None] - centres[:, None, :]
    direct_sq = jnp.sum(diff * diff, axis=0)
    mirrored = centre_mine[2][:, None] + centres[2][None, :]
    image_sq = diff[0] * diff[0] + diff[1] * diff[1] + mirrored * mirrored
    kernel = 1.0 / jnp.sqrt(direct_sq + 1.0) + 1.0 / jnp.sqrt(image_sq + 1.0)
    gap = jnp.abs(my_bubbles[:, None] - jnp.arange(centres.shape[1])[None, :])
    return jnp.where(gap > reach, kernel, jnp.zeros_like(kernel))


def per_device(
    density,
    right_side,
    inv_diag,
    near_vals,
    near_bubble,
    near_block,
    near_count,
    colour,
    moment_map,
    spread_map,
    centres,
):
    bub_dev = density.shape[0]
    panels_dev = density.shape[1]
    block_size = inv_diag.shape[2]
    my_index = lax.axis_index("bubble")
    my_bubbles = my_index * bub_dev + jnp.arange(bub_dev, dtype=jnp.int32)
    first_bubble = my_index * bub_dev - bub_dev
    kernel = far_kernel(centres, my_bubbles, bub_dev)
    relaxed = density
    for colour_now in range(2):
        dens_bf = relaxed.astype(jnp.bfloat16)
        panel_full = lax.all_gather(dens_bf, "panel", axis=1, tiled=True)
        neighbourhood = with_halo(panel_full, (("bubble", 0),), bub_dev)
        near = near_field(
            neighbourhood, near_vals, near_bubble, near_block, near_count, first_bubble, block_size
        )
        partial_value = jnp.einsum(
            "bki,bi->bk", moment_map, dens_bf, preferred_element_type=jnp.float32
        )
        own_moments = lax.psum(partial_value, "panel")
        all_moments = lax.all_gather(own_moments, "bubble", axis=0, tiled=True)
        far_coeff = jnp.dot(kernel, all_moments, precision=lax.Precision.HIGHEST).astype(
            jnp.bfloat16
        )
        far = jnp.einsum("bki,bk->bi", spread_map, far_coeff, preferred_element_type=jnp.float32)
        remainder = (right_side - near.reshape(bub_dev, panels_dev) - far).astype(jnp.bfloat16)
        remainder = remainder.reshape(bub_dev, panels_dev // block_size, block_size)
        updated = jnp.einsum(
            "brij,brj->bri", inv_diag, remainder, preferred_element_type=jnp.float32
        )
        relaxed = jnp.where(
            (colour == colour_now)[:, None], updated.reshape(bub_dev, panels_dev), relaxed
        )
    return relaxed


def solution(mesh):
    in_specs = (
        P("bubble", "panel"),
        P("bubble", "panel"),
        P("bubble", "panel", None, None),
        P("bubble", "panel", None, None, None),
        P("bubble", "panel", None),
        P("bubble", "panel", None),
        P("bubble", "panel"),
        P("bubble"),
        P("bubble", None, "panel"),
        P("bubble", None, "panel"),
        P(),
    )
    out_specs = P("bubble", "panel")
    return jax.shard_map(
        per_device, mesh=mesh, in_specs=in_specs, out_specs=out_specs, check_vma=False
    )
```

profile of v0, /device:TPU:24, one launch (start us, length us, event | category | flops | bytes accessed | tf_op | source)
XLA Modules:
  0.0 213.0 jit_solution(4248419762880765899)
XLA Ops:
  0.0 0.9 convert_element_type.18
  0.9 19.4 %all_gather.12 = bf16[8,12288]{1,0:T(8,128)(2,1)S(1)} all-gather(bf16[8,768]{1,0:T(8,128)(2,1)S(1)} %convert_element_type.18), channel_id=1, replica_groups=mesh['bubble'=16,'panel'=16] {'panel'}, dimensions={1}, use_global_device_ids=true | all-gather | bytes 208896 | tf_op jit(solution)/shard_map/all_gather | solution.py:66
  20.2 3.8 %collective-permute-start = (bf16[8,12288]{1,0:T(8,128)(2,1)S(1)}, bf16[8,12288]{1,0:T(8,128)(2,1)S(1)}, u32[]{:S(2)}, u32[]{:S(2)}) collective-permute-start(bf16[8,12288]{1,0:T(8,128)(2,1)S(1)} %all_gather.12), channel_id=1, source_target_pairs={{0,16},{16,32},{32,48},{48,64},{64,80},{80,96},{96,112},{112,128},... | collective-permute-start | bytes 589832 | tf_op jit(solution)/shard_map/ppermute | solution.py:14
  24.0 6.2 %collective-permute-start.1 = (bf16[8,12288]{1,0:T(8,128)(2,1)S(1)}, bf16[8,12288]{1,0:T(8,128)(2,1)S(1)}, u32[]{:S(2)}, u32[]{:S(2)}) collective-permute-start(bf16[8,12288]{1,0:T(8,128)(2,1)S(1)} %all_gather.12), channel_id=1, source_target_pairs={{16,0},{32,16},{48,32},{64,48},{80,64},{96,80},{112,96},{128,112},... | collective-permute-start | bytes 589832 | tf_op jit(solution)/shard_map/ppermute | solution.py:15
  30.3 0.8 copy.18
  31.1 0.6 gather_fusion.1
  31.7 0.1 copy.19
  31.8 0.2 slice_reduce_fusion
  31.9 0.7 slice_bitcast_fusion
  32.6 0.7 convert_bitcast_fusion
  33.4 0.8 multiply_reduce_fusion
  34.1 1.1 fusion.16
  35.2 27.2 %psum.14 = f32[8,16]{1,0:T(8,128)S(1)} all-reduce(f32[8,16]{1,0:T(8,128)S(1)} %bitcast.107), channel_id=1, replica_groups=mesh['bubble'=16,'panel'=16] {'panel'}, use_global_device_ids=true, to_apply=%region_1.2 | all-reduce | flops 128 | bytes 1024 | tf_op jit(solution)/shard_map/psum | solution.py:74
  62.4 37.8 %all_gather.13 = f32[128,16]{1,0:T(8,128)S(1)} all-gather(f32[8,16]{1,0:T(8,128)S(1)} %psum.14), channel_id=1, replica_groups=mesh['bubble'=16,'panel'=16] {'bubble'}, dimensions={0}, use_global_device_ids=true | all-gather | bytes 8704 | tf_op jit(solution)/shard_map/all_gather | solution.py:75
  100.2 0.7 fusion.22
  101.0 0.1 copy.17
  101.1 0.1 reshape.62
  101.2 0.8 iota_compare_fusion
  101.9 0.1 fusion.31
  102.0 0.2 fusion
  102.2 1.1 fusion.34
  103.3 0.7 broadcast_compare_fusion.1
  103.9 0.0 collective-permute-done
  103.9 0.0 collective-permute-done.1
  104.0 0.1 copy.36
  104.1 2.5 %gather_fusion = bf16[192,128]{1,0:T(8,128)(2,1)S(1)} fusion(bf16[24,96,128]{2,1,0:T(8,128)(2,1)S(1)} %bitcast.101, s32[192]{0:T(256)S(1)} %reshape.62), kind=kCustom, calls=%fused_computation | custom fusion | bytes 99840 | tf_op jit(solution)/shard_map/gather | solution.py:26
  106.6 0.1 select_bitcast_fusion.1
  106.7 0.0 copy-start.3
  106.8 4.5 %fusion.4 = f32[8,6,1,128,1]{3,2,4,1,0:T(1,128)S(1)} fusion(bf16[8,6,4,128,128]{4,3,2,1,0:T(8,128)(2,1)} %param.14, bf16[8,6,4,128,1]{3,2,1,0,4:T(4,128)(2,1)S(1)} %select_bitcast_fusion.1), kind=kOutput, calls=%fused_computation.11 | convolution fusion | flops 6291456 | bytes 6365184 | tf_op jit(solution)/shard_map/brsij,brsj->bri/dot_general | solution.py:29
  111.3 0.0 copy-start.1
  111.3 0.9 fusion.14
  112.2 0.1 fusion.36
  112.3 16.5 %all_gather.14 = bf16[8,12288]{1,0:T(8,128)(2,1)S(1)} all-gather(bf16[8,768]{1,0:T(8,128)(2,1)S(1)} %fusion.36), channel_id=1, replica_groups=mesh['bubble'=16,'panel'=16] {'panel'}, dimensions={1}, use_global_device_ids=true | all-gather | bytes 208896 | tf_op jit(solution)/shard_map/all_gather | solution.py:66
  128.8 2.0 collective-permute-start.2
  130.8 7.5 %collective-permute-start.3 = (bf16[8,12288]{1,0:T(8,128)(2,1)S(1)}, bf16[8,12288]{1,0:T(8,128)(2,1)S(1)}, u32[]{:S(2)}, u32[]{:S(2)}) collective-permute-start(bf16[8,12288]{1,0:T(8,128)(2,1)S(1)} %all_gather.14), channel_id=1, source_target_pairs={{16,0},{32,16},{48,32},{64,48},{80,64},{96,80},{112,96},{128,112},... | collective-permute-start | bytes 589832 | tf_op jit(solution)/shard_map/ppermute | solution.py:15
  138.3 0.2 fusion.12
  138.4 28.5 %psum.15 = f32[8,16]{1,0:T(8,128)S(1)} all-reduce(f32[8,16]{1,0:T(8,128)S(1)} %bitcast.108), channel_id=1, replica_groups=mesh['bubble'=16,'panel'=16] {'panel'}, use_global_device_ids=true, to_apply=%region_2.3 | all-reduce | flops 128 | bytes 1024 | tf_op jit(solution)/shard_map/psum | solution.py:74
  166.9 36.7 %all_gather.15 = f32[128,16]{1,0:T(8,128)S(1)} all-gather(f32[8,16]{1,0:T(8,128)S(1)} %psum.15), channel_id=1, replica_groups=mesh['bubble'=16,'panel'=16] {'bubble'}, dimensions={0}, use_global_device_ids=true | all-gather | bytes 8704 | tf_op jit(solution)/shard_map/all_gather | solution.py:75
  203.7 0.2 fusion.1
  203.8 0.2 fusion.32
  204.0 0.0 collective-permute-done.2
  204.0 0.0 collective-permute-done.3
  204.1 0.1 copy.37
  204.2 2.5 %gather_fusion.2 = bf16[192,128]{1,0:T(8,128)(2,1)S(1)} fusion(bf16[24,96,128]{2,1,0:T(8,128)(2,1)S(1)} %bitcast.100, s32[192]{0:T(256)S(1)} %reshape.62), kind=kCustom, calls=%fused_computation.2 | custom fusion | bytes 99840 | tf_op jit(solution)/shard_map/gather | solution.py:26
  206.7 0.1 select_bitcast_fusion
  206.8 4.5 %fusion.2 = f32[8,6,1,128,1]{3,2,4,1,0:T(1,128)S(1)} fusion(bf16[8,6,4,128,128]{4,3,2,1,0:T(8,128)(2,1)} %param.14, bf16[8,6,4,128,1]{3,2,1,0,4:T(4,128)(2,1)S(1)} %select_bitcast_fusion), kind=kOutput, calls=%fused_computation.9 | convolution fusion | flops 6291456 | bytes 6365184 | tf_op jit(solution)/shard_map/brsij,brsj->bri/dot_general | solution.py:29
  211.3 0.9 fusion.10
  212.3 0.7 bitcast_select_fusion
  (15 shorter events, 0.1 us)
Async XLA Ops:
  0.0 111.3 %copy-start = (bf16[8,6,128,128]{3,2,1,0:T(8,128)(2,1)S(1)}, bf16[8,6,128,128]{3,2,1,0:T(8,128)(2,1)}, u32[]{:S(2)}) copy-start(bf16[8,6,128,128]{3,2,1,0:T(8,128)(2,1)} %param.13) | copy-start | bytes 4718596
  20.2 83.7 %collective-permute-start = (bf16[8,12288]{1,0:T(8,128)(2,1)S(1)}, bf16[8,12288]{1,0:T(8,128)(2,1)S(1)}, u32[]{:S(2)}, u32[]{:S(2)}) collective-permute-start(bf16[8,12288]{1,0:T(8,128)(2,1)S(1)} %all_gather.12), channel_id=1, source_target_pairs={{0,16},{16,32},{32,48},{48,64},{64,80},{80,96},{96,112},{112,128},... | collective-permute-start | bytes 589832 | tf_op jit(solution)/shard_map/ppermute | solution.py:14
  24.0 79.9 %collective-permute-start.1 = (bf16[8,12288]{1,0:T(8,128)(2,1)S(1)}, bf16[8,12288]{1,0:T(8,128)(2,1)S(1)}, u32[]{:S(2)}, u32[]{:S(2)}) collective-permute-start(bf16[8,12288]{1,0:T(8,128)(2,1)S(1)} %all_gather.12), channel_id=1, source_target_pairs={{16,0},{32,16},{48,32},{64,48},{80,64},{96,80},{112,96},{128,112},... | collective-permute-start | bytes 589832 | tf_op jit(solution)/shard_map/ppermute | solution.py:15
  106.7 4.5 %copy-start.3 = (f32[8,768]{1,0:T(8,128)S(1)}, f32[8,768]{1,0:T(8,128)}, u32[]{:S(2)}) copy-start(f32[8,768]{1,0:T(8,128)} %param.12) | copy-start | bytes 73732
  111.3 1.0 copy-start.2
  111.3 27.0 %copy-start.4 = (bf16[8,16,768]{2,1,0:T(8,128)(2,1)S(1)}, bf16[8,16,768]{2,1,0:T(8,128)(2,1)}, u32[]{:S(2)}) copy-start(bf16[8,16,768]{2,1,0:T(8,128)(2,1)} %param.19) | copy-start | bytes 589828
  111.3 92.5 %copy-start.1 = (bf16[8,16,768]{2,1,0:T(8,128)(2,1)S(1)}, bf16[8,16,768]{2,1,0:T(8,128)(2,1)}, u32[]{:S(2)}) copy-start(bf16[8,16,768]{2,1,0:T(8,128)(2,1)} %param.20) | copy-start | bytes 589828
  128.8 75.2 %collective-permute-start.2 = (bf16[8,12288]{1,0:T(8,128)(2,1)S(1)}, bf16[8,12288]{1,0:T(8,128)(2,1)S(1)}, u32[]{:S(2)}, u32[]{:S(2)}) collective-permute-start(bf16[8,12288]{1,0:T(8,128)(2,1)S(1)} %all_gather.14), channel_id=1, source_target_pairs={{0,16},{16,32},{32,48},{48,64},{64,80},{80,96},{96,112},{112,128},... | collective-permute-start | bytes 589832 | tf_op jit(solution)/shard_map/ppermute | solution.py:14
  130.8 73.2 %collective-permute-start.3 = (bf16[8,12288]{1,0:T(8,128)(2,1)S(1)}, bf16[8,12288]{1,0:T(8,128)(2,1)S(1)}, u32[]{:S(2)}, u32[]{:S(2)}) collective-permute-start(bf16[8,12288]{1,0:T(8,128)(2,1)S(1)} %all_gather.14), channel_id=1, source_target_pairs={{16,0},{32,16},{48,32},{64,48},{80,64},{96,80},{112,96},{128,112},... | collective-permute-start | bytes 589832 | tf_op jit(solution)/shard_map/ppermute | solution.py:15
where the time goes:
time: 214 us; the launch traced here: 213 us
  blocking collectives  166 us (78%)
  starting transfers between devices  19.5 us (9%)
  matrix products  13.6 us (6%)
  local copies, waits for them, and re-layouts  7.75 us (4%)
  other arithmetic  5.75 us (3%)
    all_gather x2, blocking collectives, per_device(): all_moments = lax.all_gather(own_moments, 'bubble', axis=0, tiled=True)  74.5 us
    psum x2, blocking collectives, per_device(): own_moments = lax.psum(partial_value, 'panel')  55.7 us
    all_gather x2, blocking collectives, per_device(): panel_full = lax.all_gather(dens_bf, 'panel', axis=1, tiled=True)  35.9 us
    ppermute x2, starting transfers between devices, with_halo(): after = lax.ppermute(first, axis, down)  13.7 us
    dot_general x2, matrix products, near_field(): jnp.einsum('brsij,brsj->bri', near_vals, sources, preferred_element_type=...  9.02 us
    ppermute x2, starting transfers between devices, with_halo(): before = lax.ppermute(last, axis, up)  5.78 us
    gather x2, local copies, waits for them, and re-layouts, near_field(): sources = blocks[local_bubble, near_block]  5.03 us
  transfers between devices with their start and end apart: 4, of which 0 were waited for; matrix products, arithmetic and copies ran while one was open for 4% of the time, Pallas kernels for 0%

commit v1 on v0

--- a/solution.py
+++ b/solution.py
@@ -71,7 +71,7 @@
         partial_value = jnp.einsum(
             "bki,bi->bk", moment_map, dens_bf, preferred_element_type=jnp.float32
         )
-        own_moments = lax.psum(partial_value, "panel")
+        own_moments = jnp.sum(lax.all_gather(partial_value, "panel"), axis=0)
         all_moments = lax.all_gather(own_moments, "bubble", axis=0, tiled=True)
         far_coeff = jnp.dot(kernel, all_moments, precision=lax.Precision.HIGHEST).astype(
             jnp.bfloat16

time: 214 us -> 193 us (0.902)
  blocking collectives: 166 us -> 144 us
    psum x2 -> x0, blocking collectives: 55.7 us -> none  [per_device(): own_moments = lax.psum(partial_value, 'panel')]
    all_gather x0 -> x2, blocking collectives: none -> 32.3 us  [per_device(): own_moments = jnp.sum(lax.all_gather(partial_value, 'panel'), axis=0)]
  transfers between devices with their start and end apart: 4 -> 4, of which waited for: 0 -> 0; matrix products, arithmetic and copies ran while one was open for 4% -> 5% of each run, Pallas kernels for 0% -> 0%
where the time goes in v1:
time: 193 us; the launch traced here: 191 us
  blocking collectives  144 us (75%)
  starting transfers between devices  19.5 us (10%)
  matrix products  13.6 us (7%)
  local copies, waits for them, and re-layouts  7.75 us (4%)
  other arithmetic  5.8 us (3%)
    all_gather x2, blocking collectives, per_device(): all_moments = lax.all_gather(own_moments, 'bubble', axis=0, tiled=True)  74.3 us
    all_gather x2, blocking collectives, per_device(): panel_full = lax.all_gather(dens_bf, 'panel', axis=1, tiled=True)  37.8 us
    all_gather x2, blocking collectives, per_device(): own_moments = jnp.sum(lax.all_gather(partial_value, 'panel'), axis=0)  32.3 us
    ppermute x2, starting transfers between devices, with_halo(): after = lax.ppermute(first, axis, down)  13.8 us
    dot_general x2, matrix products, near_field(): jnp.einsum('brsij,brsj->bri', near_vals, sources, preferred_element_type=...  9.02 us
    ppermute x2, starting transfers between devices, with_halo(): before = lax.ppermute(last, axis, up)  5.73 us
    gather x2, local copies, waits for them, and re-layouts, near_field(): sources = blocks[local_bubble, near_block]  5.03 us
  transfers between devices with their start and end apart: 4, of which 0 were waited for; matrix products, arithmetic and copies ran while one was open for 5% of the time, Pallas kernels for 0%

profile of v1, /device:TPU:24, one launch (start us, length us, event | category | flops | bytes accessed | tf_op | source)
XLA Modules:
  0.0 191.3 jit_solution(16642784593482714770)
XLA Ops:
  0.0 0.9 convert_element_type.18
  0.9 19.4 %all_gather.24 = bf16[8,12288]{1,0:T(8,128)(2,1)S(1)} all-gather(bf16[8,768]{1,0:T(8,128)(2,1)S(1)} %convert_element_type.18), channel_id=1, replica_groups=mesh['bubble'=16,'panel'=16] {'panel'}, dimensions={1}, use_global_device_ids=true | all-gather | bytes 208896 | tf_op jit(solution)/shard_map/all_gather | solution.py:66
  20.2 3.8 %collective-permute-start = (bf16[8,12288]{1,0:T(8,128)(2,1)S(1)}, bf16[8,12288]{1,0:T(8,128)(2,1)S(1)}, u32[]{:S(2)}, u32[]{:S(2)}) collective-permute-start(bf16[8,12288]{1,0:T(8,128)(2,1)S(1)} %all_gather.24), channel_id=1, source_target_pairs={{0,16},{16,32},{32,48},{48,64},{64,80},{80,96},{96,112},{112,128},... | collective-permute-start | bytes 589832 | tf_op jit(solution)/shard_map/ppermute | solution.py:14
  24.0 6.2 %collective-permute-start.1 = (bf16[8,12288]{1,0:T(8,128)(2,1)S(1)}, bf16[8,12288]{1,0:T(8,128)(2,1)S(1)}, u32[]{:S(2)}, u32[]{:S(2)}) collective-permute-start(bf16[8,12288]{1,0:T(8,128)(2,1)S(1)} %all_gather.24), channel_id=1, source_target_pairs={{16,0},{32,16},{48,32},{64,48},{80,64},{96,80},{112,96},{128,112},... | collective-permute-start | bytes 589832 | tf_op jit(solution)/shard_map/ppermute | solution.py:15
  30.3 0.8 copy.18
  31.1 0.6 gather_fusion.1
  31.7 0.1 copy.19
  31.8 0.2 slice_reduce_fusion
  31.9 0.7 slice_bitcast_fusion
  32.6 0.7 convert_bitcast_fusion
  33.4 0.8 multiply_reduce_fusion
  34.1 1.1 fusion.16
  35.2 16.2 %all-gather = f32[128,16]{1,0:T(8,128)S(1)} all-gather(f32[8,16]{1,0:T(8,128)S(1)} %bitcast.111), channel_id=2, replica_groups=mesh['bubble'=16,'panel'=16] {'panel'}, dimensions={0}, use_global_device_ids=true | all-gather | bytes 8704 | tf_op jit(solution)/shard_map/all_gather | solution.py:74
  51.4 37.8 %all_gather.27 = f32[128,16]{1,0:T(8,128)S(1)} all-gather(f32[8,16]{1,0:T(8,128)S(1)} %bitcast_reduce_fusion.1), channel_id=1, replica_groups=mesh['bubble'=16,'panel'=16] {'bubble'}, dimensions={0}, use_global_device_ids=true | all-gather | bytes 8704 | tf_op jit(solution)/shard_map/all_gather | solution.py:75
  89.2 0.7 fusion.22
  90.0 0.1 copy.17
  90.1 0.1 reshape.62
  90.2 0.8 iota_compare_fusion
  91.0 0.1 fusion.31
  91.0 0.2 fusion
  91.2 1.1 fusion.34
  92.3 0.7 broadcast_compare_fusion.1
  93.0 0.0 collective-permute-done
  93.0 0.0 collective-permute-done.1
  93.0 0.1 copy.36
  93.1 2.5 %gather_fusion = bf16[192,128]{1,0:T(8,128)(2,1)S(1)} fusion(bf16[24,96,128]{2,1,0:T(8,128)(2,1)S(1)} %bitcast.105, s32[192]{0:T(256)S(1)} %reshape.62), kind=kCustom, calls=%fused_computation | custom fusion | bytes 99840 | tf_op jit(solution)/shard_map/gather | solution.py:26
  95.6 0.1 select_bitcast_fusion.1
  95.7 0.0 copy-start.3
  95.8 4.5 %fusion.4 = f32[8,6,1,128,1]{3,2,4,1,0:T(1,128)S(1)} fusion(bf16[8,6,4,128,128]{4,3,2,1,0:T(8,128)(2,1)} %param.14, bf16[8,6,4,128,1]{3,2,1,0,4:T(4,128)(2,1)S(1)} %select_bitcast_fusion.1), kind=kOutput, calls=%fused_computation.11 | convolution fusion | flops 6291456 | bytes 6365184 | tf_op jit(solution)/shard_map/brsij,brsj->bri/dot_general | solution.py:29
  100.3 0.0 copy-start.1
  100.3 0.9 fusion.14
  101.2 0.1 fusion.36
  101.3 18.4 %all_gather.28 = bf16[8,12288]{1,0:T(8,128)(2,1)S(1)} all-gather(bf16[8,768]{1,0:T(8,128)(2,1)S(1)} %fusion.36), channel_id=1, replica_groups=mesh['bubble'=16,'panel'=16] {'panel'}, dimensions={1}, use_global_device_ids=true | all-gather | bytes 208896 | tf_op jit(solution)/shard_map/all_gather | solution.py:66
  119.8 1.9 collective-permute-start.2
  121.7 7.5 %collective-permute-start.3 = (bf16[8,12288]{1,0:T(8,128)(2,1)S(1)}, bf16[8,12288]{1,0:T(8,128)(2,1)S(1)}, u32[]{:S(2)}, u32[]{:S(2)}) collective-permute-start(bf16[8,12288]{1,0:T(8,128)(2,1)S(1)} %all_gather.28), channel_id=1, source_target_pairs={{16,0},{32,16},{48,32},{64,48},{80,64},{96,80},{112,96},{128,112},... | collective-permute-start | bytes 589832 | tf_op jit(solution)/shard_map/ppermute | solution.py:15
  129.2 0.2 fusion.12
  129.4 16.1 %all-gather.1 = f32[128,16]{1,0:T(8,128)S(1)} all-gather(f32[8,16]{1,0:T(8,128)S(1)} %bitcast.112), channel_id=3, replica_groups=mesh['bubble'=16,'panel'=16] {'panel'}, dimensions={0}, use_global_device_ids=true | all-gather | bytes 8704 | tf_op jit(solution)/shard_map/all_gather | solution.py:74
  145.5 36.5 %all_gather.31 = f32[128,16]{1,0:T(8,128)S(1)} all-gather(f32[8,16]{1,0:T(8,128)S(1)} %bitcast_reduce_fusion), channel_id=1, replica_groups=mesh['bubble'=16,'panel'=16] {'bubble'}, dimensions={0}, use_global_device_ids=true | all-gather | bytes 8704 | tf_op jit(solution)/shard_map/all_gather | solution.py:75
  182.0 0.2 fusion.1
  182.1 0.2 fusion.32
  182.3 0.0 collective-permute-done.2
  182.3 0.1 maximum_bitcast_fusion.1
  182.4 0.1 copy.37
  182.5 2.5 %gather_fusion.2 = bf16[192,128]{1,0:T(8,128)(2,1)S(1)} fusion(bf16[24,96,128]{2,1,0:T(8,128)(2,1)S(1)} %bitcast.104, s32[192]{0:T(256)S(1)} %reshape.62), kind=kCustom, calls=%fused_computation.2 | custom fusion | bytes 99840 | tf_op jit(solution)/shard_map/gather | solution.py:26
  185.0 0.1 select_bitcast_fusion
  185.1 4.5 %fusion.2 = f32[8,6,1,128,1]{3,2,4,1,0:T(1,128)S(1)} fusion(bf16[8,6,4,128,128]{4,3,2,1,0:T(8,128)(2,1)} %param.14, bf16[8,6,4,128,1]{3,2,1,0,4:T(4,128)(2,1)S(1)} %select_bitcast_fusion), kind=kOutput, calls=%fused_computation.9 | convolution fusion | flops 6291456 | bytes 6365184 | tf_op jit(solution)/shard_map/brsij,brsj->bri/dot_general | solution.py:29
  189.7 0.9 fusion.10
  190.6 0.7 bitcast_select_fusion
  (17 shorter events, 0.1 us)
Async XLA Ops:
  0.0 100.3 %copy-start = (bf16[8,6,128,128]{3,2,1,0:T(8,128)(2,1)S(1)}, bf16[8,6,128,128]{3,2,1,0:T(8,128)(2,1)}, u32[]{:S(2)}) copy-start(bf16[8,6,128,128]{3,2,1,0:T(8,128)(2,1)} %param.13) | copy-start | bytes 4718596
  20.2 72.7 %collective-permute-start = (bf16[8,12288]{1,0:T(8,128)(2,1)S(1)}, bf16[8,12288]{1,0:T(8,128)(2,1)S(1)}, u32[]{:S(2)}, u32[]{:S(2)}) collective-permute-start(bf16[8,12288]{1,0:T(8,128)(2,1)S(1)} %all_gather.24), channel_id=1, source_target_pairs={{0,16},{16,32},{32,48},{48,64},{64,80},{80,96},{96,112},{112,128},... | collective-permute-start | bytes 589832 | tf_op jit(solution)/shard_map/ppermute | solution.py:14
  24.0 68.9 %collective-permute-start.1 = (bf16[8,12288]{1,0:T(8,128)(2,1)S(1)}, bf16[8,12288]{1,0:T(8,128)(2,1)S(1)}, u32[]{:S(2)}, u32[]{:S(2)}) collective-permute-start(bf16[8,12288]{1,0:T(8,128)(2,1)S(1)} %all_gather.24), channel_id=1, source_target_pairs={{16,0},{32,16},{48,32},{64,48},{80,64},{96,80},{112,96},{128,112},... | collective-permute-start | bytes 589832 | tf_op jit(solution)/shard_map/ppermute | solution.py:15
  95.7 4.5 %copy-start.3 = (f32[8,768]{1,0:T(8,128)S(1)}, f32[8,768]{1,0:T(8,128)}, u32[]{:S(2)}) copy-start(f32[8,768]{1,0:T(8,128)} %param.12) | copy-start | bytes 73732
  100.3 1.0 copy-start.2
  100.3 28.9 %copy-start.4 = (bf16[8,16,768]{2,1,0:T(8,128)(2,1)S(1)}, bf16[8,16,768]{2,1,0:T(8,128)(2,1)}, u32[]{:S(2)}) copy-start(bf16[8,16,768]{2,1,0:T(8,128)(2,1)} %param.19) | copy-start | bytes 589828
  100.3 81.9 %copy-start.1 = (bf16[8,16,768]{2,1,0:T(8,128)(2,1)S(1)}, bf16[8,16,768]{2,1,0:T(8,128)(2,1)}, u32[]{:S(2)}) copy-start(bf16[8,16,768]{2,1,0:T(8,128)(2,1)} %param.20) | copy-start | bytes 589828
  119.8 62.6 %collective-permute-start.2 = (bf16[8,12288]{1,0:T(8,128)(2,1)S(1)}, bf16[8,12288]{1,0:T(8,128)(2,1)S(1)}, u32[]{:S(2)}, u32[]{:S(2)}) collective-permute-start(bf16[8,12288]{1,0:T(8,128)(2,1)S(1)} %all_gather.28), channel_id=1, source_target_pairs={{0,16},{16,32},{32,48},{48,64},{64,80},{80,96},{96,112},{112,128},... | collective-permute-start | bytes 589832 | tf_op jit(solution)/shard_map/ppermute | solution.py:14
  121.7 60.7 %collective-permute-start.3 = (bf16[8,12288]{1,0:T(8,128)(2,1)S(1)}, bf16[8,12288]{1,0:T(8,128)(2,1)S(1)}, u32[]{:S(2)}, u32[]{:S(2)}) collective-permute-start(bf16[8,12288]{1,0:T(8,128)(2,1)S(1)} %all_gather.28), channel_id=1, source_target_pairs={{16,0},{32,16},{48,32},{64,48},{80,64},{96,80},{112,96},{128,112},... | collective-permute-start | bytes 589832 | tf_op jit(solution)/shard_map/ppermute | solution.py:15
